TPU v7x, 128 devices: a whole 4x4x4 slice. The times are simulated.
128 devices in a mesh: row: 8 (over x, y_lo), col: 16 (over z, y_hi, core).
Axes of the slice: x: 4, y: 4 (y_hi: 2, y_lo: 2; y = y_hi * 2 + y_lo), z: 4, core: 2. Of those that a mesh axis runs over, the one named last changes fastest.
Arguments:
- atom_blocks: float32 [128, 16, 128, 128], P('row', 'col'), may hold values from -6 to 6
- grid_position: int32 [128], replicated, may hold values from 0 to 127, as said below
- pattern: int32 [128, 16], replicated, may hold values from -1 to 127, as said below
Outputs:
- square: float32 [128, 16, 128, 128], P('row', 'col')
- update: float32 [128, 16, 128, 128], P('row', 'col')
Inputs may be any that keep to these rules, and one draw needn't show every extreme that they name: grid_position is a permutation; the 16 atom block rows a with a // 16 equal put at most 2 grid positions into any one run of 16 grid positions that starts at a multiple of 16, and exactly 2 into some run. `pattern`: each row holds 12 different block columns, one of them its own index, and -1 in its other slots; all slots s that hold one block column j have the same s; the block rows lie on a cycle of 128 places, not given, on which each row's columns lie within 16 places in a row around its own.
All inputs are finite; a program needn't handle non-finite values.
Results may differ from a plain program's by a relative error of at most 0.0003.
Values sent between devices are 32-bit elements; how exact they have to be, the bound alone decides.
No kernel may reach another device: no remote copies, remote signals or barrier semaphores. Data moves between devices by JAX's collectives and lax.ppermute only.
A program may use at most 128 MiB of HBM per device.

v0:
```python
import math
import jax
import jax.numpy as jnp
from jax import lax
from jax.sharding import PartitionSpec as P

NZ = 12
HIGHEST = lax.Precision.HIGHEST


def atoms_of_rows(grid_position, grid_rows):
    atom_numbers = jnp.arange(grid_position.shape[0], dtype=jnp.int32)
    hits = grid_position[None, :] == grid_rows[:, None]
    return jnp.sum(jnp.where(hits, atom_numbers[None, :], 0), axis=1)


def on_device(atom_blocks, grid_position, pattern):
    group_rows = atom_blocks.shape[0]
    local_slots = atom_blocks.shape[1]
    block_edge = atom_blocks.shape[2]
    row_count = lax.axis_size("row")
    row_index = lax.axis_index("row")
    column_index = lax.axis_index("col")
    local_rows = jnp.arange(group_rows, dtype=jnp.int32)
    grid_rows = row_index * group_rows + local_rows
    grid_atoms = atoms_of_rows(grid_position, grid_rows)
    capacity = 2 * ((group_rows + 2 * row_count - 1) // (2 * row_count))
    local_place = lax.dynamic_slice_in_dim(grid_position, row_index * group_rows, group_rows)
    target = local_place // group_rows
    ranking = jnp.sum(
        (target[None, :] == target[:, None]) & (local_rows[None, :] < local_rows[:, None]), axis=1
    )
    slot_code = target * capacity + ranking
    flat_slots = jnp.arange(row_count * capacity, dtype=jnp.int32)
    source = jnp.sum(
        jnp.where(slot_code[None, :] == flat_slots[:, None], local_rows[None, :], 0), axis=1
    )
    outgoing = jnp.take(atom_blocks, source, axis=0).reshape(
        row_count, capacity, local_slots, block_edge, block_edge
    )
    incoming = lax.all_to_all(outgoing, "row", split_axis=0, concat_axis=0, tiled=True)
    source_group = grid_atoms // group_rows
    within = grid_atoms % group_rows
    group_targets = (grid_position // group_rows).reshape(row_count, group_rows)
    their_targets = jnp.take(group_targets, source_group, axis=0)
    arrival = jnp.sum(
        (their_targets == row_index) & (local_rows[None, :] < within[:, None]), axis=1
    )
    slot_index = source_group * capacity + arrival
    arrived = incoming.reshape(row_count * capacity, local_slots, block_edge, block_edge)
    grid_blocks = jnp.take(arrived, slot_index, axis=0)
    grid_pattern = jnp.take(pattern, grid_atoms, axis=0)
    own_pattern = lax.dynamic_slice_in_dim(grid_pattern, column_index * local_slots, local_slots, 1)
    own_filled = own_pattern >= 0
    column_pattern = lax.dynamic_slice_in_dim(pattern, column_index * local_slots, local_slots, 1)
    start_scale = 1.0 / math.sqrt(NZ * block_edge)
    scale_back = math.sqrt(NZ * block_edge)
    matrix = jnp.where(own_filled[:, :, None, None], grid_blocks * start_scale, 0.0)

    def contribution(panel_part, right_panel):
        neighbours = jnp.maximum(grid_pattern, 0)
        right_rows = jnp.take(right_panel, jnp.take(grid_position, neighbours), axis=0)
        right_pattern = jnp.take(column_pattern, neighbours, axis=0)
        matches = (
            (right_pattern[:, :, :, None] == own_pattern[:, None, None, :])
            & own_filled[:, None, None, :]
            & (grid_pattern >= 0)[:, :, None, None]
        )
        weights = jnp.where(matches[:, :, 0, :, None, None], right_rows[:, :, 0][:, :, None], 0.0)
        return jnp.einsum("iupq,iutqr->itpr", panel_part, weights, precision=HIGHEST)

    def multiply(right_panel):
        return contribution(lax.all_gather(matrix, "col", axis=1, tiled=True), right_panel)

    right_panel = lax.all_gather(matrix, "row", axis=0, tiled=True)
    masked_square = multiply(right_panel)
    square_panel = lax.all_gather(masked_square, "row", axis=0, tiled=True)
    cubic = multiply(square_panel)
    square = masked_square * scale_back
    update = (1.5 * matrix - 0.5 * cubic) * scale_back
    return (square, update)


def solution(mesh):
    in_specs = (P("row", "col", None, None), P(), P())
    out_specs = (P("row", "col", None, None), P("row", "col", None, None))
    return jax.shard_map(
        on_device, mesh=mesh, in_specs=in_specs, out_specs=out_specs, check_vma=False
    )
```

profile of v0, /device:TPU:5, one launch (start us, length us, event | category | flops | bytes accessed | tf_op | source)
XLA Modules:
  0.0 577.1 jit_solution(7751069718583219607)
XLA Ops:
  7.2 0.9 select_reduce_fusion.1
  8.1 0.7 and_select_fusion.3
  8.9 0.2 convert_reduce_fusion.1
  9.1 0.7 multiply_add_fusion
  9.8 0.1 select_reduce_fusion
  10.0 0.6 gather_fusion.3
  10.6 1.1 bitcast_select_fusion.1
  11.7 5.3 all-to-all-start
  17.0 0.7 and_select_fusion.1
  17.8 0.8 copy.41
  18.6 0.1 fusion.32
  18.7 0.6 gather_fusion.1
  19.3 0.6 gather_fusion
  19.9 0.2 compare_reduce_fusion
  20.1 0.2 convert_reduce_fusion
  20.3 10.3 %all-to-all-done = f32[8,2,1,128,128]{4,3,1,2,0:T(8,128)S(1)} async-done(((f32[8,2,1,128,128]{4,3,1,2,0:T(8,128)}), f32[8,2,1,128,128]{4,3,1,2,0:T(8,128)S(1)}, u32[]{:S(2)}, u32[]{:S(2)}) %all-to-all-start) | async-done | bytes 1048608 | tf_op jit(solution)/shard_map/all_to_all | solution.py:41
  30.7 0.6 gather_fusion.4
  31.3 1.2 fusion.31
  32.6 0.7 all-gather.6.cloned.1.call-update
  33.4 1.9 gather_fusion.5
  35.3 0.7 dynamic-slice_bitcast_fusion
  36.0 1.9 gather_fusion.2
  38.0 0.2 dynamic-slice_reduce_fusion
  38.4 169.3 %all-gather.4.cloned.1.call-done = f32[128,1,128,128]{3,2,1,0:T(8,128)} async-done(((f32[16,1,128,128]{3,2,1,0:T(8,128)}), f32[128,1,128,128]{3,2,1,0:T(8,128)}) %all-gather.4.cloned.1.call-update) | async-done | bytes 8388624 | tf_op jit(solution)/shard_map/all_gather | solution.py:75
  207.7 15.6 %gather_fusion.6 = f32[256,128,128]{2,1,0:T(8,128)} fusion(f32[128,128,128]{2,1,0:T(8,128)} %bitcast.69, s32[1024]{0:T(1024)S(1)} %pad_clamp_fusion), kind=kCustom, calls=%fused_computation.3.clone | custom fusion | bytes 33555456 | tf_op jit(solution)/shard_map/jit(_take)/gather | solution.py:62
  223.2 18.0 %copy.45 = f32[16,16,1,128,128]{3,4,1,0,2:T(8,128)} copy(f32[16,16,1,128,128]{4,3,1,0,2:T(8,128)} %bitcast.68) | data formatting | bytes 33554432 | tf_op jit(solution)/shard_map/jit(_take)/gather | solution.py:62
  241.2 80.1 %all-gather.6.cloned.1.call-done = f32[16,16,128,128]{3,2,1,0:T(8,128)} async-done(((f32[16,1,128,128]{3,2,1,0:T(8,128)}), f32[16,16,128,128]{3,2,1,0:T(8,128)}) %all-gather.6.cloned.1.call-update) | async-done | bytes 16777232 | tf_op jit(solution)/shard_map/all_gather | solution.py:73
  321.4 23.0 %broadcast_multiply_fusion = (f32[16,1,128,128]{3,2,1,0:T(8,128)}, f32[16,1,128,128]{3,2,1,0:T(8,128)}) fusion(f32[16,16,128,128]{3,2,1,0:T(8,128)} %all-gather.6.cloned.1.call-done, f32[16,16,1,128,128]{3,4,1,0,2:T(8,128)} %copy.45, pred[16,16]{1,0:T(8,128)(4,1)S(1)} %get-tuple-element.8, pred[16,16]{1,0:T(8,128)(4,1)S(1)} %get-tuple-element.16), kind=kOutput, calls=%fused_computation.32 | convolution fusion | flops 6451101696 | bytes 35652096 | tf_op jit(solution)/shard_map/iupq,iutqr->itpr/dot_general | solution.py:70
  344.4 170.2 %all-gather.8.cloned.1.call-done = f32[128,1,128,128]{3,2,1,0:T(8,128)} async-done(((f32[16,1,128,128]{3,2,1,0:T(8,128)}), f32[128,1,128,128]{3,2,1,0:T(8,128)}) %all-gather.8.cloned.1.call-update) | async-done | bytes 8388624 | tf_op jit(solution)/shard_map/all_gather | solution.py:77
  514.6 15.4 %gather_fusion.7 = f32[256,128,128]{2,1,0:T(8,128)} fusion(f32[128,128,128]{2,1,0:T(8,128)} %bitcast.70, s32[1024]{0:T(1024)S(1)} %pad_clamp_fusion), kind=kCustom, calls=%fused_computation.5.clone | custom fusion | bytes 33555456 | tf_op jit(solution)/shard_map/jit(_take)/gather | solution.py:62
  530.0 17.8 %copy.47 = f32[16,16,1,128,128]{3,4,1,0,2:T(8,128)} copy(f32[16,16,1,128,128]{4,3,1,0,2:T(8,128)} %bitcast.67) | data formatting | bytes 33554432 | tf_op jit(solution)/shard_map/jit(_take)/gather | solution.py:62
  547.8 22.8 %fusion.27 = f32[16,1,128,128]{3,2,1,0:T(8,128)} fusion(f32[16,16,128,128]{3,2,1,0:T(8,128)} %all-gather.6.cloned.1.call-done, f32[16,16,1,128,128]{3,4,1,0,2:T(8,128)} %copy.47, pred[16,16]{1,0:T(8,128)(4,1)S(1)} %get-tuple-element.8, pred[16,16]{1,0:T(8,128)(4,1)S(1)} %get-tuple-element.16, f32[16,1,128,128]{3,2,1,0:T(8,128)S(1)} %copy-done.3), kind=kOutput, calls=%fused_computation.27 | convolution fusion | flops 6451888128 | bytes 35652096 | tf_op jit(solution)/shard_map/iupq,iutqr->itpr/dot_general | solution.py:70
  (30 shorter events, 0.9 us)
Async XLA Ops:
  7.2 2.8 copy-start
  7.2 26.2 %copy-start.2 = (s32[128]{0:T(128)S(1)}, s32[128]{0:T(128)}, u32[]{:S(2)}) copy-start(s32[128]{0:T(128)} %param.12) | copy-start | bytes 1540
  11.7 19.0 %all-to-all-start = ((f32[8,2,1,128,128]{4,3,1,2,0:T(8,128)}), f32[8,2,1,128,128]{4,3,1,2,0:T(8,128)S(1)}, u32[]{:S(2)}, u32[]{:S(2)}) async-start(f32[8,2,1,128,128]{4,3,1,2,0:T(8,128)} %bitcast.5), calls=%async_computation | async-start | bytes 2097152 | tf_op jit(solution)/shard_map/all_to_all | solution.py:41
  17.0 190.7 %all-gather.4.cloned.1.call-start = ((), (), s32[]{:S(2)}) async-start(), calls=%async_computation.1 | async-start | bytes 9437184 | tf_op jit(solution)/shard_map/all_gather | solution.py:75
  32.5 288.8 %all-gather.6.cloned.1.call-start = ((), (), s32[]{:S(2)}) async-start(), calls=%async_computation.2 | async-start | bytes 17825792 | tf_op jit(solution)/shard_map/all_gather | solution.py:73
  33.3 481.4 %all-gather.8.cloned.1.call-start = ((), (), s32[]{:S(2)}) async-start(), calls=%async_computation.3 | async-start | bytes 9437184 | tf_op jit(solution)/shard_map/all_gather | solution.py:77
  530.0 17.8 %copy-start.3 = (f32[16,1,128,128]{3,2,1,0:T(8,128)S(1)}, f32[16,1,128,128]{3,2,1,0:T(8,128)}, u32[]{:S(2)}) copy-start(f32[16,1,128,128]{3,2,1,0:T(8,128)} %fusion.31) | copy-start | bytes 3145732
  530.0 40.6 %copy-start.1 = (f32[16,1,128,128]{3,2,1,0:T(8,128)S(1)}, f32[16,1,128,128]{3,2,1,0:T(8,128)}, u32[]{:S(2)}) copy-start(f32[16,1,128,128]{3,2,1,0:T(8,128)} %param.11) | copy-start | bytes 3145732
Sparse Core Ops, SparseCore 0:
  32.6 174.9 all-gather.3
  210.7 110.6 all-gather.5
  344.6 170.0 all-gather.7
where the time goes:
time: 578 us; the launch traced here: 577 us
  waiting for transfers between devices  431 us (75%)
  local copies, waits for them, and re-layouts  75 us (13%)
  matrix products  45.9 us (8%)
  between operations  13.9 us (2%)
  other arithmetic  6.41 us (1%)
    all_gather x1, waiting for transfers between devices, on_device(): square_panel = lax.all_gather(masked_square, 'row', axis=0, tiled=True)  170 us
    all_gather x1, waiting for transfers between devices, on_device(): right_panel = lax.all_gather(matrix, 'row', axis=0, tiled=True)  169 us
    all_gather x1, waiting for transfers between devices, multiply(): lax.all_gather(matrix, 'col', axis=1, tiled=True)  80.1 us
    gather x4, local copies, waits for them, and re-layouts, contribution(): jnp.take(right_panel, jnp.take(grid_position, neighbours), axis=0)  66.7 us
    dot_general x2, matrix products, contribution(): jnp.einsum('iupq,iutqr->itpr', panel_part, weights, precision=HIGHEST)  45.9 us
  transfers between devices with their start and end apart: 4, of which 4 were waited for; matrix products, arithmetic and copies ran while one was open for 7% of the time, Pallas kernels for 0%

commit v1 on v0

--- a/solution.py
+++ b/solution.py
@@ -1,3 +1,4 @@
+import functools
 import math
 import jax
 import jax.numpy as jnp
@@ -6,6 +7,18 @@
 
 NZ = 12
 HIGHEST = lax.Precision.HIGHEST
+
+
+def pair_field(sample, array_axis):
+    return jnp.concatenate(
+        lax.all_to_all(
+            jnp.stack([sample] * lax.axis_size("row")), axis_name="row", split_axis=0, concat_axis=0
+        ),
+        axis=array_axis,
+    )
+
+
+_lift_node = functools.partial(pair_field, array_axis=0)
 
 
 def atoms_of_rows(grid_position, grid_rows):
@@ -74,7 +87,7 @@
 
     right_panel = lax.all_gather(matrix, "row", axis=0, tiled=True)
     masked_square = multiply(right_panel)
-    square_panel = lax.all_gather(masked_square, "row", axis=0, tiled=True)
+    square_panel = _lift_node(masked_square)
     cubic = multiply(square_panel)
     square = masked_square * scale_back
     update = (1.5 * matrix - 0.5 * cubic) * scale_back

time: 578 us -> 507 us (0.88)
  waiting for transfers between devices: 431 us -> 260 us
  blocking collectives: 0 us -> 95.6 us
    all_gather x1 -> x0, waiting for transfers between devices: 170 us -> none  [on_device(): square_panel = lax.all_gather(masked_square, 'row', axis=0, tiled=True)]
    all_to_all x0 -> x1, blocking collectives: none -> 95.6 us  [pair_field(): lax.all_to_all(jnp.stack([sample] * lax.axis_size('row')), axis_name='row...]
  transfers between devices with their start and end apart: 4 -> 3, of which waited for: 4 -> 3; matrix products, arithmetic and copies ran while one was open for 7% -> 8% of each run, Pallas kernels for 0% -> 0%
where the time goes in v1:
time: 507 us; the launch traced here: 503 us
  waiting for transfers between devices  260 us (51%)
  blocking collectives  95.6 us (19%)
  local copies, waits for them, and re-layouts  75.8 us (15%)
  matrix products  45.4 us (9%)
  between operations  14.2 us (3%)
  other arithmetic  6.41 us (1%)
  starting transfers between devices  5.3 us (1%)
    all_gather x1, waiting for transfers between devices, on_device(): right_panel = lax.all_gather(matrix, 'row', axis=0, tiled=True)  169 us
    all_to_all x1, blocking collectives, pair_field(): lax.all_to_all(jnp.stack([sample] * lax.axis_size('row')), axis_name='row...  95.6 us
    all_gather x1, waiting for transfers between devices, multiply(): lax.all_gather(matrix, 'col', axis=1, tiled=True)  80.1 us
    gather x4, local copies, waits for them, and re-layouts, contribution(): jnp.take(right_panel, jnp.take(grid_position, neighbours), axis=0)  66.5 us
    dot_general x2, matrix products, contribution(): jnp.einsum('iupq,iutqr->itpr', panel_part, weights, precision=HIGHEST)  45.4 us
    all_to_all x1, waiting for transfers between devices, on_device(): lax.all_to_all(outgoing, 'row', split_axis=0, concat_axis=0, tiled=True)  10.3 us
  transfers between devices with their start and end apart: 3, of which 3 were waited for; matrix products, arithmetic and copies ran while one was open for 8% of the time, Pallas kernels for 0%

profile of v1, /device:TPU:5, one launch (start us, length us, event | category | flops | bytes accessed | tf_op | source)
XLA Modules:
  0.0 503.1 jit_solution(15175456770669681130)
XLA Ops:
  7.2 0.9 select_reduce_fusion.1
  8.1 0.7 and_select_fusion.3
  8.9 0.2 convert_reduce_fusion.1
  9.1 0.7 multiply_add_fusion
  10.0 0.6 gather_fusion.3
  10.6 1.1 bitcast_select_fusion.1
  11.7 5.3 %all-to-all-start = ((f32[8,2,1,128,128]{4,3,1,2,0:T(8,128)}), f32[8,2,1,128,128]{4,3,1,2,0:T(8,128)S(1)}, u32[]{:S(2)}, u32[]{:S(2)}) async-start(f32[8,2,1,128,128]{4,3,1,2,0:T(8,128)} %bitcast.5), calls=%async_computation | async-start | bytes 2097152 | tf_op jit(solution)/shard_map/all_to_all | solution.py:54
  17.0 0.7 and_select_fusion.1
  17.8 0.8 copy.40
  18.6 0.1 fusion.29
  18.7 0.6 gather_fusion.1
  19.3 0.6 gather_fusion
  19.9 0.2 compare_reduce_fusion
  20.1 0.2 convert_reduce_fusion
  20.3 10.3 %all-to-all-done = f32[8,2,1,128,128]{4,3,1,2,0:T(8,128)S(1)} async-done(((f32[8,2,1,128,128]{4,3,1,2,0:T(8,128)}), f32[8,2,1,128,128]{4,3,1,2,0:T(8,128)S(1)}, u32[]{:S(2)}, u32[]{:S(2)}) %all-to-all-start) | async-done | bytes 1048608 | tf_op jit(solution)/shard_map/all_to_all | solution.py:54
  30.7 0.6 gather_fusion.4
  31.3 1.2 fusion.28
  32.6 0.7 all-gather.5.cloned.1.call-update
  33.4 1.9 gather_fusion.5
  35.2 0.7 dynamic-slice_bitcast_fusion
  35.9 1.9 gather_fusion.2
  38.0 0.2 dynamic-slice_reduce_fusion
  38.3 169.3 %all-gather.3.cloned.1.call-done = f32[128,1,128,128]{3,2,1,0:T(8,128)} async-done(((f32[16,1,128,128]{3,2,1,0:T(8,128)}), f32[128,1,128,128]{3,2,1,0:T(8,128)}) %all-gather.3.cloned.1.call-update) | async-done | bytes 8388624 | tf_op jit(solution)/shard_map/all_gather | solution.py:88
  207.7 15.6 %gather_fusion.6 = f32[256,128,128]{2,1,0:T(8,128)} fusion(f32[128,128,128]{2,1,0:T(8,128)} %bitcast.72, s32[1024]{0:T(1024)S(1)} %pad_clamp_fusion), kind=kCustom, calls=%fused_computation.3.clone | custom fusion | bytes 33555456 | tf_op jit(solution)/shard_map/jit(_take)/gather | solution.py:75
  223.2 18.0 %copy.44 = f32[16,16,1,128,128]{3,4,1,0,2:T(8,128)} copy(f32[16,16,1,128,128]{4,3,1,0,2:T(8,128)} %bitcast.71) | data formatting | bytes 33554432 | tf_op jit(solution)/shard_map/jit(_take)/gather | solution.py:75
  241.2 80.1 %all-gather.5.cloned.1.call-done = f32[16,16,128,128]{3,2,1,0:T(8,128)} async-done(((f32[16,1,128,128]{3,2,1,0:T(8,128)}), f32[16,16,128,128]{3,2,1,0:T(8,128)}) %all-gather.5.cloned.1.call-update) | async-done | bytes 16777232 | tf_op jit(solution)/shard_map/all_gather | solution.py:86
  321.3 22.7 %bitcast_multiply_fusion = (f32[16,1,128,128]{3,2,1,0:T(8,128)}, f32[16,128,128,1]{1,2,3,0:T(8,128)S(1)}) fusion(f32[16,16,128,128]{3,2,1,0:T(8,128)} %all-gather.5.cloned.1.call-done, f32[16,16,1,128,128]{3,4,1,0,2:T(8,128)} %copy.44, pred[16,16]{1,0:T(8,128)(4,1)S(1)} %get-tuple-element.8, pred[16,16]{1,0:T(8,128)(4,1)S(1)} %get-tuple-element.16), kind=kOutput, calls=%fused_computation.27 | convolution fusion | flops 6451101696 | bytes 35652096 | tf_op jit(solution)/shard_map/iupq,iutqr->itpr/dot_general | solution.py:83
  344.0 1.0 stack.2
  345.1 95.6 %all_to_all.10 = f32[8,16,1,128,128]{4,3,1,2,0:T(8,128)} all-to-all(f32[8,16,1,128,128]{4,3,1,2,0:T(8,128)S(1)} %stack.2), channel_id=1, replica_groups=mesh['row'=8,'col'=16] {'row'}, dimensions={0} | all-to-all | bytes 16777216 | tf_op jit(solution)/shard_map/all_to_all | solution.py:14
  440.6 15.2 %gather_fusion.7 = f32[256,128,128]{2,1,0:T(8,128)} fusion(f32[128,128,128]{2,1,0:T(8,128)} %bitcast.69, s32[1024]{0:T(1024)S(1)} %pad_clamp_fusion), kind=kCustom, calls=%fused_computation.5.clone | custom fusion | bytes 33555456 | tf_op jit(solution)/shard_map/jit(_take)/gather | solution.py:75
  455.8 17.8 %copy.46 = f32[16,16,1,128,128]{3,4,1,0,2:T(8,128)} copy(f32[16,16,1,128,128]{4,3,1,0,2:T(8,128)} %bitcast.70) | data formatting | bytes 33554432 | tf_op jit(solution)/shard_map/jit(_take)/gather | solution.py:75
  473.6 22.7 %fusion.24 = f32[16,1,128,128]{3,2,1,0:T(8,128)} fusion(f32[16,16,128,128]{3,2,1,0:T(8,128)} %all-gather.5.cloned.1.call-done, f32[16,16,1,128,128]{3,4,1,0,2:T(8,128)} %copy.46, pred[16,16]{1,0:T(8,128)(4,1)S(1)} %get-tuple-element.8, pred[16,16]{1,0:T(8,128)(4,1)S(1)} %get-tuple-element.16, f32[16,1,128,128]{3,2,1,0:T(8,128)S(1)} %copy-done.3), kind=kOutput, calls=%fused_computation.26 | convolution fusion | flops 6451888128 | bytes 35652096 | tf_op jit(solution)/shard_map/iupq,iutqr->itpr/dot_general | solution.py:83
  (29 shorter events, 0.9 us)
Async XLA Ops:
  7.2 2.8 copy-start
  7.2 26.2 %copy-start.2 = (s32[128]{0:T(128)S(1)}, s32[128]{0:T(128)}, u32[]{:S(2)}) copy-start(s32[128]{0:T(128)} %param.12) | copy-start | bytes 1540
  11.7 19.0 %all-to-all-start = ((f32[8,2,1,128,128]{4,3,1,2,0:T(8,128)}), f32[8,2,1,128,128]{4,3,1,2,0:T(8,128)S(1)}, u32[]{:S(2)}, u32[]{:S(2)}) async-start(f32[8,2,1,128,128]{4,3,1,2,0:T(8,128)} %bitcast.5), calls=%async_computation | async-start | bytes 2097152 | tf_op jit(solution)/shard_map/all_to_all | solution.py:54
  17.0 190.7 %all-gather.3.cloned.1.call-start = ((), (), s32[]{:S(2)}) async-start(), calls=%async_computation.2 | async-start | bytes 9437184 | tf_op jit(solution)/shard_map/all_gather | solution.py:88
  32.5 288.8 %all-gather.5.cloned.1.call-start = ((), (), s32[]{:S(2)}) async-start(), calls=%async_computation.3 | async-start | bytes 17825792 | tf_op jit(solution)/shard_map/all_gather | solution.py:86
  455.8 17.8 %copy-start.3 = (f32[16,1,128,128]{3,2,1,0:T(8,128)S(1)}, f32[16,1,128,128]{3,2,1,0:T(8,128)}, u32[]{:S(2)}) copy-start(f32[16,1,128,128]{3,2,1,0:T(8,128)} %fusion.28) | copy-start | bytes 3145732
  455.8 40.5 %copy-start.1 = (f32[16,1,128,128]{3,2,1,0:T(8,128)S(1)}, f32[16,1,128,128]{3,2,1,0:T(8,128)}, u32[]{:S(2)}) copy-start(f32[16,1,128,128]{3,2,1,0:T(8,128)} %param.11) | copy-start | bytes 3145732
Sparse Core Ops, SparseCore 0:
  32.6 174.9 all-gather.2
  210.7 110.6 all-gather.4
